TPU v7x, 512 devices: a whole 4x4x16 slice. The times are simulated.
512 devices in a mesh: dp: 16 (over x, y), heads: 16 (over z), side: 2 (over core).
Axes of the slice: x: 4, y: 4, z: 16, core: 2. Of those that a mesh axis runs over, the one named last changes fastest.
Arguments:
- queries: bfloat16 [384, 2, 4096], P('dp', None, ('heads', 'side')), may hold values from -6 to 6
- new_keys: bfloat16 [384, 2, 4096], P('dp', None, ('heads', 'side')), may hold values from -6 to 6
- new_values: bfloat16 [384, 2, 4096], P('dp', None, ('heads', 'side')), may hold values from -6 to 6
- head_states: bfloat16 [384, 32, 128, 128], P('dp', ('heads', 'side')), may hold values from -6 to 6
- slopes: float32 [32], P(('heads', 'side')), may hold values from 0.004 to 0.9
- head_gain: float32 [4096], P(('heads', 'side')), may hold values from 0.5 to 1.5
- out_weight: bfloat16 [4096, 3072], P(('heads', 'side')), may hold values from -0.1875 to 0.1875
- residual: bfloat16 [384, 2, 3072], P('dp', None, ('heads', 'side')), may hold values from -10 to 10
- norm_gain: float32 [3072], replicated, may hold values from 0.5 to 1.5
- expert_ids: int32 [384, 2, 2], P('dp'), may hold values from 0 to 15, all different within a row; in each aligned block of 48 rows (0 to 47, 48 to 95, ..., all dimensions but the last counted through in order) at most 9 rows name the same one
- expert_gates: float32 [384, 2, 2], P('dp'), may hold values from 0.2 to 1
- w_gate: bfloat16 [16, 16, 192, 4608], P('dp', None, 'side', 'heads'), may hold values from -0.109375 to 0.109375
- w_up: bfloat16 [16, 16, 192, 4608], P('dp', None, 'side', 'heads'), may hold values from -0.109375 to 0.109375
- w_down: bfloat16 [16, 4608, 16, 192], P('dp', 'heads', None, 'side'), may hold values from -0.125 to 0.125
Outputs:
- state_out: bfloat16 [384, 32, 128, 128], P('dp', ('heads', 'side'))
- resid_out: bfloat16 [384, 2, 3072], P('dp', None, ('heads', 'side'))
- moe_out: bfloat16 [384, 2, 3072], P('dp', None, ('heads', 'side'))
Inputs may be any that keep to these rules, and one draw needn't show every extreme that they name: `expert_ids`: among the 48 tokens of one dp index a token's 2 experts differ, no expert is chosen by more than 9 of them, and some expert is chosen by exactly 9.
All inputs are finite; a program needn't handle non-finite values.
Results may differ from a plain program's by a relative error of at most 0.025.
Values may be sent and summed in bfloat16 or wider, within the bound.
A program may use at most 64 MiB of HBM per device.

v0:
```python
import jax
import jax.numpy as jnp
from jax import lax
from jax.sharding import PartitionSpec as P


def local(
    queries,
    new_keys,
    new_values,
    head_states,
    slopes,
    head_gain,
    out_weight,
    residual,
    norm_gain,
    expert_ids,
    expert_gates,
    w_gate,
    w_up,
    w_down,
):
    requests_dev, step_count, inner_width = queries.shape
    local_heads = slopes.shape[0]
    head_size = inner_width // local_heads
    query_rows = queries.astype(jnp.float32).reshape(
        requests_dev, step_count, local_heads, head_size
    )
    key_rows = new_keys.astype(jnp.float32).reshape(
        requests_dev, step_count, local_heads, head_size
    )
    value_rows = new_values.astype(jnp.float32).reshape(
        requests_dev, step_count, local_heads, head_size
    )
    decays = jnp.exp(-slopes)[None, :, None, None]
    current = head_states.astype(jnp.float32)
    outputs = []
    for step in range(step_count):
        current = decays * current + key_rows[:, step, :, :, None] * value_rows[:, step, :, None, :]
        outputs.append(
            jnp.einsum(
                "rhi,rhij->rhj", query_rows[:, step], current, precision=lax.Precision.HIGHEST
            )
        )
    state_out = current.astype(jnp.bfloat16)
    head_output = jnp.stack(outputs, 1)
    scaled = head_output * lax.rsqrt(jnp.mean(head_output * head_output, -1, keepdims=True) + 1e-06)
    tokens_dev = requests_dev * step_count
    normed = (
        (scaled * head_gain.reshape(local_heads, head_size))
        .astype(jnp.bfloat16)
        .reshape(tokens_dev, inner_width)
    )
    partial_out = jnp.dot(normed, out_weight, preferred_element_type=jnp.float32)
    attention = lax.psum_scatter(partial_out, ("heads", "side"), scatter_dimension=1, tiled=True)
    width = norm_gain.shape[0]
    piece_width = attention.shape[1]
    resid_new = (residual.reshape(tokens_dev, piece_width).astype(jnp.float32) + attention).astype(
        jnp.bfloat16
    )
    stream = resid_new.astype(jnp.float32)
    sum_squares = lax.psum(jnp.sum(stream * stream, 1), ("heads", "side"))
    gain_piece = lax.dynamic_slice_in_dim(
        norm_gain, lax.axis_index(("heads", "side")) * piece_width, piece_width
    )
    mixed_in = (stream * lax.rsqrt(sum_squares / width + 1e-06)[:, None] * gain_piece).astype(
        jnp.bfloat16
    )
    groups = lax.axis_size("dp")
    heads_count = lax.axis_size("heads")
    choices_each = expert_ids.shape[2]
    capacity = max(2, 3 * choices_each * tokens_dev // (2 * groups))
    flat_ids = expert_ids.reshape(-1)
    onehot_table = (flat_ids[:, None] == jnp.arange(groups, dtype=jnp.int32)[None, :]).astype(
        jnp.int32
    )
    earlier = jnp.cumsum(onehot_table, 0) - onehot_table
    slot_index = jnp.sum(earlier * onehot_table, 1)
    target = flat_ids * capacity + slot_index
    source_row = jnp.arange(tokens_dev * choices_each, dtype=jnp.int32) // choices_each
    gate_flat = w_gate[0].reshape(-1, w_gate.shape[3])
    up_flat = w_up[0].reshape(-1, w_up.shape[3])
    down_flat = w_down[0].reshape(w_down.shape[1], -1)
    holder = jnp.zeros((groups * capacity, mixed_in.shape[1]), mixed_in.dtype)
    arrived = lax.all_to_all(
        holder.at[target].set(mixed_in[source_row]).reshape(groups, capacity, mixed_in.shape[1]),
        "dp",
        split_axis=0,
        concat_axis=0,
        tiled=True,
    )
    piece = lax.all_gather(arrived, "heads", axis=2, tiled=True)
    flat_piece = piece.reshape(-1, piece.shape[2])
    gate_part = jnp.dot(flat_piece, gate_flat, preferred_element_type=jnp.float32)
    up_part = jnp.dot(flat_piece, up_flat, preferred_element_type=jnp.float32)
    gate_val, up_val = (
        lax.psum(gate_part.astype(jnp.bfloat16), "side").astype(jnp.float32),
        lax.psum(up_part.astype(jnp.bfloat16), "side").astype(jnp.float32),
    )
    activation = (jax.nn.silu(gate_val) * up_val).astype(jnp.bfloat16)
    down_part = jnp.dot(activation, down_flat, preferred_element_type=jnp.float32).reshape(
        groups, capacity, heads_count, piece_width
    )
    reduced = lax.psum_scatter(
        down_part.astype(jnp.bfloat16), "heads", scatter_dimension=2, tiled=True
    )
    returned = lax.all_to_all(reduced, "dp", split_axis=0, concat_axis=0, tiled=True)
    picked = returned.reshape(groups * capacity, piece_width)[target].astype(jnp.float32)
    weighted = picked * expert_gates.reshape(-1)[:, None]
    moe_out = jnp.sum(weighted.reshape(tokens_dev, choices_each, piece_width), 1).astype(
        jnp.bfloat16
    )
    return (
        state_out,
        resid_new.reshape(requests_dev, step_count, piece_width),
        moe_out.reshape(requests_dev, step_count, piece_width),
    )


def solution(mesh):
    return jax.shard_map(
        local,
        mesh=mesh,
        in_specs=(
            P("dp", None, ("heads", "side")),
            P("dp", None, ("heads", "side")),
            P("dp", None, ("heads", "side")),
            P("dp", ("heads", "side"), None, None),
            P(("heads", "side")),
            P(("heads", "side")),
            P(("heads", "side"), None),
            P("dp", None, ("heads", "side")),
            P(),
            P("dp", None, None),
            P("dp", None, None),
            P("dp", None, "side", "heads"),
            P("dp", None, "side", "heads"),
            P("dp", "heads", None, "side"),
        ),
        out_specs=(
            P("dp", ("heads", "side"), None, None),
            P("dp", None, ("heads", "side")),
            P("dp", None, ("heads", "side")),
        ),
        check_vma=False,
    )
```

profile of v0, /device:TPU:32, one launch (start us, length us, event | category | flops | bytes accessed | tf_op | source)
XLA Modules:
  0.0 491.2 jit_solution(13953203980056573112)
XLA Ops:
  7.2 0.8 bitcast_convert_fusion.1
  10.3 2.2 fusion.5
  12.5 1.8 fusion.8
  14.6 1.6 convolution_bitcast_fusion
  17.0 0.8 dynamic_slice.3
  17.9 110.4 %reduce-scatter.7.cloned.1.call-done = f32[96,48]{1,0:T(8,128)} async-done(((f32[3072,48]{1,0:T(8,128)}), f32[96,48]{1,0:T(8,128)}) %reduce-scatter.7.cloned.1.call-update) | async-done | bytes 18448
  128.3 0.9 copy.61
  129.3 46.0 %psum.21 = f32[48]{0:T(128)S(1)} all-reduce(f32[48]{0:T(128)S(1)} %get-tuple-element.5), channel_id=1, replica_groups=mesh['dp'=16,'heads'=16,'side'=2] {'heads','side'}, use_global_device_ids=true, to_apply=%region_5.6 | all-reduce | flops 48 | bytes 384 | tf_op jit(solution)/shard_map/psum | solution.py:62
  175.4 1.0 scatter_custom_fusion
  176.6 14.1 %all_to_all.10 = bf16[16,2,432]{2,1,0:T(2,128)(2,1)S(1)} all-to-all(bf16[16,2,432]{2,1,0:T(2,128)(2,1)S(1)} %reshape.300), channel_id=1, replica_groups=mesh['dp'=16,'heads'=16,'side'=2] {'dp'}, dimensions={0} | all-to-all | bytes 55296 | tf_op jit(solution)/shard_map/all_to_all | solution.py:85
  191.2 83.1 %all_gather.3 = bf16[16,9,1536]{1,0,2:T(8,128)(2,1)} all-gather(bf16[16,9,96]{1,0,2:T(8,128)(2,1)S(1)} %copy.44), channel_id=1, replica_groups=mesh['dp'=16,'heads'=16,'side'=2] {'heads'}, dimensions={2}, use_global_device_ids=true | all-gather | bytes 470016 | tf_op jit(solution)/shard_map/all_gather | solution.py:92
  274.3 8.2 %reshape.288 = bf16[144,1536]{0,1:T(8,128)(2,1)S(1)} reshape(bf16[16,9,1536]{1,0,2:T(8,128)(2,1)} %all_gather.3) | data formatting | bytes 884736 | tf_op jit(solution)/shard_map/reshape | solution.py:93
  282.5 1.1 convolution_convert_fusion.1
  283.8 1.1 convolution_convert_fusion.2
  285.0 2.4 reshape_squeeze.11
  288.1 36.6 %all-reduce.7.cloned.1.call-done = (bf16[144,288]{1,0:T(8,128)(2,1)}, bf16[144,288]{1,0:T(8,128)(2,1)}) async-done(((bf16[144,288]{1,0:T(8,128)(2,1)}, bf16[144,288]{1,0:T(8,128)(2,1)}), (bf16[144,288]{1,0:T(8,128)(2,1)}, bf16[144,288]{1,0:T(8,128)(2,1)})) %all-reduce.7.cloned.1.call-update) | async-done | bytes 165904 | tf_op jit(solution)/shard_map/psum | solution.py:98
  324.7 1.0 fusion.23
  325.8 1.6 convolution_convert_fusion
  327.4 1.3 dynamic-slice
  328.7 1.7 fusion.4
  330.5 136.0 %all-reduce.5.cloned.1.call-done = bf16[16,9,16,96]{3,0,2,1:T(8,128)(2,1)} async-done(((bf16[16,9,16,96]{3,0,2,1:T(8,128)(2,1)}), bf16[16,9,16,96]{3,0,2,1:T(8,128)(2,1)}) %all-reduce.5.cloned.1.call-update) | async-done | bytes 442384
  466.5 1.4 constant_dynamic-slice_fusion
  468.6 6.8 %all-to-all-start.1 = ((bf16[16,2,432]{2,1,0:T(2,128)(2,1)}), bf16[16,2,432]{2,1,0:T(2,128)(2,1)S(1)}, u32[]{:S(2)}, u32[]{:S(2)}) async-start(bf16[16,2,432]{2,1,0:T(2,128)(2,1)} %reshape.302), calls=%async_computation.1 | async-start | bytes 65536 | tf_op jit(solution)/shard_map/all_to_all | solution.py:107
  475.6 7.5 %all-to-all-done.1 = bf16[16,2,432]{2,1,0:T(2,128)(2,1)S(1)} async-done(((bf16[16,2,432]{2,1,0:T(2,128)(2,1)}), bf16[16,2,432]{2,1,0:T(2,128)(2,1)S(1)}, u32[]{:S(2)}, u32[]{:S(2)}) %all-to-all-start.1) | async-done | bytes 27680 | tf_op jit(solution)/shard_map/all_to_all | solution.py:107
  (62 shorter events, 7.0 us)
Async XLA Ops:
  7.2 275.4 %copy-start = (bf16[1,16,96,288]{3,2,1,0:T(8,128)(2,1)S(1)}, bf16[1,16,96,288]{3,2,1,0:T(8,128)(2,1)}, u32[]{:S(2)}) copy-start(bf16[1,16,96,288]{3,2,1,0:T(8,128)(2,1)} %param.26) | copy-start | bytes 2654212
  7.2 5.3 %copy-start.2 = (bf16[24,1,128,128]{3,2,1,0:T(8,128)(2,1)S(1)}, bf16[24,1,128,128]{3,2,1,0:T(8,128)(2,1)}, u32[]{:S(2)}) copy-start(bf16[24,1,128,128]{3,2,1,0:T(8,128)(2,1)} %param.17) | copy-start | bytes 2359300
  7.2 121.1 %reduce-scatter.7.cloned.1.call-start = ((), (), s32[]{:S(2)}) async-start(), calls=%async_computation.3 | async-start | bytes 1622016
  12.5 2.0 copy-start.4
  12.5 2.1 copy-start.9
  14.5 1.7 copy-start.7
  16.2 113.0 %copy-start.6 = (bf16[24,2,96]{2,1,0:T(2,128)(2,1)S(1)}, bf16[24,2,96]{2,1,0:T(2,128)(2,1)}, u32[]{:S(2)}) copy-start(bf16[24,2,96]{2,1,0:T(2,128)(2,1)} %param.21) | copy-start | bytes 27652
  16.2 308.5 %all-reduce.7.cloned.1.call-start = ((), (), s32[]{:S(2)}) async-start(), calls=%async_computation.5 | async-start | bytes 442368 | tf_op jit(solution)/shard_map/psum | solution.py:98
  129.3 145.0 %copy-start.5 = (bf16[48,96]{1,0:T(8,128)(2,1)}, bf16[48,96]{1,0:T(8,128)(2,1)S(1)}, u32[]{:S(2)}) copy-start(bf16[48,96]{1,0:T(8,128)(2,1)S(1)} %get-tuple-element.6) | copy-start | bytes 27652
  282.5 1.3 copy-start.1
  284.9 181.6 %all-reduce.5.cloned.1.call-start = ((), (), s32[]{:S(2)}) async-start(), calls=%async_computation.4 | async-start | bytes 1179648
  288.0 40.7 %copy-start.3 = (bf16[24,1,128,128]{3,2,1,0:T(8,128)(2,1)S(1)}, bf16[24,1,128,128]{3,2,1,0:T(8,128)(2,1)}, u32[]{:S(2)}) copy-start(bf16[24,1,128,128]{3,2,1,0:T(8,128)(2,1)} %param.17) | copy-start | bytes 2359300
  327.4 148.1 %copy-start.8 = (f32[24,2,2]{0,2,1:T(2,128)S(1)}, f32[24,2,2]{0,2,1:T(2,128)}, u32[]{:S(2)}) copy-start(f32[24,2,2]{0,2,1:T(2,128)} %param.24) | copy-start | bytes 1156
  468.6 14.4 %all-to-all-start.1 = ((bf16[16,2,432]{2,1,0:T(2,128)(2,1)}), bf16[16,2,432]{2,1,0:T(2,128)(2,1)S(1)}, u32[]{:S(2)}, u32[]{:S(2)}) async-start(bf16[16,2,432]{2,1,0:T(2,128)(2,1)} %reshape.302), calls=%async_computation.1 | async-start | bytes 65536 | tf_op jit(solution)/shard_map/all_to_all | solution.py:107
Sparse Core Ops, SparseCore 0:
  16.3 111.9 reduce-scatter.6
  285.0 39.6 all-reduce.6
  327.5 138.9 all-reduce.4
where the time goes:
time: 492 us; the launch traced here: 491 us
  waiting for transfers between devices  291 us (59%)
  blocking collectives  143 us (29%)
  local copies, waits for them, and re-layouts  20.6 us (4%)
  between operations  14.7 us (3%)
  matrix products  9.36 us (2%)
  starting transfers between devices  6.93 us (1%)
  other arithmetic  5.83 us (1%)
    unnamed x5, waiting for transfers between devices  246 us
    all_gather x1, blocking collectives, local(): piece = lax.all_gather(arrived, 'heads', axis=2, tiled=True)  83.1 us
    psum x1, blocking collectives, local(): sum_squares = lax.psum(jnp.sum(stream * stream, 1), ('heads', 'side'))  46 us
    psum x1, waiting for transfers between devices, local(): lax.psum(up_part.astype(jnp.bfloat16), 'side').astype(jnp.float32)  36.6 us
    all_to_all x1, blocking collectives, local(): lax.all_to_all(holder.at[target].set(mixed_in[source_row]).reshape(groups...  14.1 us
  transfers between devices with their start and end apart: 4, of which 4 were waited for; matrix products, arithmetic and copies ran while one was open for 2% of the time, Pallas kernels for 0%

commit v1 on v0

--- a/solution.py
+++ b/solution.py
@@ -89,7 +89,10 @@
         concat_axis=0,
         tiled=True,
     )
-    piece = lax.all_gather(arrived, "heads", axis=2, tiled=True)
+    size = lax.axis_size("heads")
+    pieces = jnp.stack([arrived for _ in range(size)])
+    pieces = lax.all_to_all(pieces, "heads", split_axis=0, concat_axis=0)
+    piece = jnp.concatenate(pieces, axis=2)
     flat_piece = piece.reshape(-1, piece.shape[2])
     gate_part = jnp.dot(flat_piece, gate_flat, preferred_element_type=jnp.float32)
     up_part = jnp.dot(flat_piece, up_flat, preferred_element_type=jnp.float32)

time: 492 us -> 434 us (0.88)
  blocking collectives: 143 us -> 105 us
  waiting for transfers between devices: 291 us -> 279 us
  local copies, waits for them, and re-layouts: 20.6 us -> 12.7 us
    all_gather x1 -> x0, blocking collectives: 83.1 us -> none  [local(): piece = lax.all_gather(arrived, 'heads', axis=2, tiled=True)]
    all_to_all x0 -> x1, blocking collectives: none -> 44.8 us  [local(): pieces = lax.all_to_all(pieces, 'heads', split_axis=0, concat_axis=0)]
    psum x1, waiting for transfers between devices: 36.6 us -> 25.4 us  [local(): lax.psum(up_part.astype(jnp.bfloat16), 'side').astype(jnp.float32)]
    reshape x1, local copies, waits for them, and re-layouts: 8.24 us -> 0.15 us  [local(): piece = jnp.concatenate(pieces, axis=2)]
where the time goes in v1:
time: 434 us
  waiting for transfers between devices  279 us (64%)
  blocking collectives  105 us (24%)
  between operations  14.7 us (3%)
  local copies, waits for them, and re-layouts  12.7 us (3%)
  matrix products  9.26 us (2%)
  starting transfers between devices  6.93 us (2%)
  other arithmetic  5.83 us (1%)
    unnamed x5, waiting for transfers between devices  247 us
    psum x1, blocking collectives, local(): sum_squares = lax.psum(jnp.sum(stream * stream, 1), ('heads', 'side'))  46 us
    all_to_all x1, blocking collectives, local(): pieces = lax.all_to_all(pieces, 'heads', split_axis=0, concat_axis=0)  44.8 us
    psum x1, waiting for transfers between devices, local(): lax.psum(up_part.astype(jnp.bfloat16), 'side').astype(jnp.float32)  25.4 us
    all_to_all x1, blocking collectives, local(): lax.all_to_all(holder.at[target].set(mixed_in[source_row]).reshape(groups...  14.1 us
  transfers between devices with their start and end apart: 4, of which 4 were waited for; matrix products, arithmetic and copies ran while one was open for 2% of the time, Pallas kernels for 0%

profile of v1, /device:TPU:32, one launch (start us, length us, event | category | flops | bytes accessed | tf_op | source)
XLA Modules:
  0.0 433.7 jit_solution(15379433573482856940)
XLA Ops:
  7.2 0.8 bitcast_convert_fusion.1
  10.3 2.2 fusion.5
  12.5 1.8 fusion.8
  14.6 1.6 convolution_bitcast_fusion
  17.0 0.8 dynamic_slice.3
  17.9 110.4 %reduce-scatter.7.cloned.1.call-done = f32[96,48]{1,0:T(8,128)} async-done(((f32[3072,48]{1,0:T(8,128)}), f32[96,48]{1,0:T(8,128)}) %reduce-scatter.7.cloned.1.call-update) | async-done | bytes 18448
  128.3 0.9 copy.59
  129.3 46.0 %psum.21 = f32[48]{0:T(128)S(1)} all-reduce(f32[48]{0:T(128)S(1)} %get-tuple-element.5), channel_id=1, replica_groups=mesh['dp'=16,'heads'=16,'side'=2] {'heads','side'}, use_global_device_ids=true, to_apply=%region_5.6 | all-reduce | flops 48 | bytes 384 | tf_op jit(solution)/shard_map/psum | solution.py:62
  175.4 1.0 scatter_custom_fusion
  176.6 14.1 %all_to_all.15 = bf16[16,2,432]{2,1,0:T(2,128)(2,1)S(1)} all-to-all(bf16[16,2,432]{2,1,0:T(2,128)(2,1)S(1)} %reshape.301), channel_id=1, replica_groups=mesh['dp'=16,'heads'=16,'side'=2] {'dp'}, dimensions={0} | all-to-all | bytes 55296 | tf_op jit(solution)/shard_map/all_to_all | solution.py:85
  190.9 44.8 %all_to_all.16 = bf16[16,16,9,96]{3,1,2,0:T(8,128)(2,1)S(1)} all-to-all(bf16[16,16,9,96]{3,1,2,0:T(8,128)(2,1)S(1)} %stack.14), channel_id=1, replica_groups=mesh['dp'=16,'heads'=16,'side'=2] {'heads'}, dimensions={0} | all-to-all | bytes 884736 | tf_op jit(solution)/shard_map/all_to_all | solution.py:94
  236.5 1.0 convolution_convert_fusion.1
  237.5 1.0 convolution_convert_fusion.2
  238.7 2.4 reshape_squeeze.11
  241.7 25.4 %all-reduce.7.cloned.1.call-done = (bf16[144,288]{1,0:T(8,128)(2,1)}, bf16[144,288]{1,0:T(8,128)(2,1)}) async-done(((bf16[144,288]{1,0:T(8,128)(2,1)}, bf16[144,288]{1,0:T(8,128)(2,1)}), (bf16[144,288]{1,0:T(8,128)(2,1)}, bf16[144,288]{1,0:T(8,128)(2,1)})) %all-reduce.7.cloned.1.call-update) | async-done | bytes 165904 | tf_op jit(solution)/shard_map/psum | solution.py:101
  267.1 1.0 fusion.23
  268.2 1.6 convolution_convert_fusion
  269.8 1.3 dynamic-slice
  271.2 1.7 fusion.4
  272.9 136.1 %all-reduce.5.cloned.1.call-done = bf16[16,9,16,96]{3,0,2,1:T(8,128)(2,1)} async-done(((bf16[16,9,16,96]{3,0,2,1:T(8,128)(2,1)}), bf16[16,9,16,96]{3,0,2,1:T(8,128)(2,1)}) %all-reduce.5.cloned.1.call-update) | async-done | bytes 442384
  409.0 1.4 constant_dynamic-slice_fusion
  411.2 6.8 %all-to-all-start.2 = ((bf16[16,2,432]{2,1,0:T(2,128)(2,1)}), bf16[16,2,432]{2,1,0:T(2,128)(2,1)S(1)}, u32[]{:S(2)}, u32[]{:S(2)}) async-start(bf16[16,2,432]{2,1,0:T(2,128)(2,1)} %reshape.303), calls=%async_computation.2 | async-start | bytes 65536 | tf_op jit(solution)/shard_map/all_to_all | solution.py:110
  418.1 7.5 %all-to-all-done.2 = bf16[16,2,432]{2,1,0:T(2,128)(2,1)S(1)} async-done(((bf16[16,2,432]{2,1,0:T(2,128)(2,1)}), bf16[16,2,432]{2,1,0:T(2,128)(2,1)S(1)}, u32[]{:S(2)}, u32[]{:S(2)}) %all-to-all-start.2) | async-done | bytes 27680 | tf_op jit(solution)/shard_map/all_to_all | solution.py:110
  426.5 0.7 fusion.25
  (64 shorter events, 6.6 us)
Async XLA Ops:
  7.2 229.3 %copy-start = (bf16[1,16,96,288]{3,2,1,0:T(8,128)(2,1)S(1)}, bf16[1,16,96,288]{3,2,1,0:T(8,128)(2,1)}, u32[]{:S(2)}) copy-start(bf16[1,16,96,288]{3,2,1,0:T(8,128)(2,1)} %param.26) | copy-start | bytes 2654212
  7.2 5.3 %copy-start.2 = (bf16[24,1,128,128]{3,2,1,0:T(8,128)(2,1)S(1)}, bf16[24,1,128,128]{3,2,1,0:T(8,128)(2,1)}, u32[]{:S(2)}) copy-start(bf16[24,1,128,128]{3,2,1,0:T(8,128)(2,1)} %param.17) | copy-start | bytes 2359300
  7.2 121.1 %reduce-scatter.7.cloned.1.call-start = ((), (), s32[]{:S(2)}) async-start(), calls=%async_computation.4 | async-start | bytes 1622016
  12.5 2.0 copy-start.4
  12.5 2.1 copy-start.9
  14.5 1.7 copy-start.7
  16.2 113.0 %copy-start.6 = (bf16[24,2,96]{2,1,0:T(2,128)(2,1)S(1)}, bf16[24,2,96]{2,1,0:T(2,128)(2,1)}, u32[]{:S(2)}) copy-start(bf16[24,2,96]{2,1,0:T(2,128)(2,1)} %param.21) | copy-start | bytes 27652
  16.2 250.9 %all-reduce.7.cloned.1.call-start = ((), (), s32[]{:S(2)}) async-start(), calls=%async_computation.6 | async-start | bytes 442368 | tf_op jit(solution)/shard_map/psum | solution.py:101
  129.3 106.5 %copy-start.5 = (bf16[48,96]{1,0:T(8,128)(2,1)}, bf16[48,96]{1,0:T(8,128)(2,1)S(1)}, u32[]{:S(2)}) copy-start(bf16[48,96]{1,0:T(8,128)(2,1)S(1)} %get-tuple-element.6) | copy-start | bytes 27652
  235.9 1.7 copy-start.1
  238.6 170.4 %all-reduce.5.cloned.1.call-start = ((), (), s32[]{:S(2)}) async-start(), calls=%async_computation.5 | async-start | bytes 1179648
  241.7 29.4 %copy-start.3 = (bf16[24,1,128,128]{3,2,1,0:T(8,128)(2,1)S(1)}, bf16[24,1,128,128]{3,2,1,0:T(8,128)(2,1)}, u32[]{:S(2)}) copy-start(bf16[24,1,128,128]{3,2,1,0:T(8,128)(2,1)} %param.17) | copy-start | bytes 2359300
  269.8 148.2 %copy-start.8 = (f32[24,2,2]{0,2,1:T(2,128)S(1)}, f32[24,2,2]{0,2,1:T(2,128)}, u32[]{:S(2)}) copy-start(f32[24,2,2]{0,2,1:T(2,128)} %param.24) | copy-start | bytes 1156
  411.2 14.4 %all-to-all-start.2 = ((bf16[16,2,432]{2,1,0:T(2,128)(2,1)}), bf16[16,2,432]{2,1,0:T(2,128)(2,1)S(1)}, u32[]{:S(2)}, u32[]{:S(2)}) async-start(bf16[16,2,432]{2,1,0:T(2,128)(2,1)} %reshape.303), calls=%async_computation.2 | async-start | bytes 65536 | tf_op jit(solution)/shard_map/all_to_all | solution.py:110
Sparse Core Ops, SparseCore 0:
  16.3 111.9 reduce-scatter.6
  238.7 28.3 all-reduce.6
  269.9 139.0 all-reduce.4
